TPU v7x, 32 devices: a whole 2x2x4 slice. The times are simulated.
32 devices in a mesh: row: 8 (over y, x, core), col: 4 (over z).
Axes of the slice: x: 2, y: 2, z: 4, core: 2. Of those that a mesh axis runs over, the one named last changes fastest.
Arguments:
- alignment: float32 [192, 16, 64], P('row', 'col'), may hold values from -6 to 6
- pair_state: float32 [192, 192, 128], P('row', 'col'), may hold values from -6 to 6
- pair_weights: float32 [8, 192, 192], P(None, 'row', 'col'), may hold values from 0 to 1, as said below
- align_gain: float32 [64], replicated, may hold values from 0.5 to 2
- value_weight: float32 [64, 256], replicated, may hold values from -0.75 to 0.75
- gate_weight: float32 [64, 256], replicated, may hold values from -0.75 to 0.75
- output_weight: float32 [256, 64], replicated, may hold values from -0.375 to 0.375
- outer_gain: float32 [64], replicated, may hold values from 0.5 to 2
- left_weight: float32 [64, 32], replicated, may hold values from -0.75 to 0.75
- right_weight: float32 [64, 32], replicated, may hold values from -0.75 to 0.75
- outer_weight: float32 [1024, 128], replicated, may hold values from -0.75 to 0.75
- outer_bias: float32 [128], replicated, may hold values from -3 to 3
Outputs:
- alignment_out: float32 [192, 16, 64], P('row', 'col')
- pair_out: float32 [192, 192, 128], P('row', 'col')
Inputs may be any that keep to these rules, and one draw needn't show every extreme that they name: `pair_weights`: every entry is positive, and for each head and row token the weights over the 192 column tokens sum to one.
All inputs are finite; a program needn't handle non-finite values.
Results may differ from a plain program's by a relative error of at most 0.00011.
Values sent between devices are 32-bit elements; how exact they have to be, the bound alone decides.
A program may use at most 64 MiB of HBM per device.

v0:
```python
import jax
import jax.numpy as jnp
from jax import lax
from jax.sharding import PartitionSpec as P

PRECISE = lax.Precision.HIGHEST


def normalize(features, channel_gain):
    channel_mean = jnp.mean(features, axis=-1, keepdims=True)
    centered = features - channel_mean
    spread = jnp.mean(centered * centered, axis=-1, keepdims=True)
    return centered * lax.rsqrt(spread + 1e-05) * channel_gain


def on_device(
    alignment,
    pair_state,
    pair_weights,
    align_gain,
    value_weight,
    gate_weight,
    output_weight,
    outer_gain,
    left_weight,
    right_weight,
    outer_weight,
    outer_bias,
):
    head_count = pair_weights.shape[0]
    local_rows = alignment.shape[0]
    local_seqs = alignment.shape[1]
    channels = alignment.shape[2]
    normed = normalize(alignment, align_gain)
    flat_normed = normed.reshape(local_rows, local_seqs * channels)
    gathered = lax.all_gather(flat_normed, "row", axis=0, tiled=True)
    gathered = gathered.reshape(-1, local_seqs, channels)
    mixed_rows = jnp.einsum(
        "hij,jsc->ishc",
        lax.all_gather(pair_weights, "col", axis=2, tiled=True),
        gathered,
        precision=PRECISE,
    )
    per_head = value_weight.reshape(channels, head_count, -1)
    averaged = jnp.einsum("ishc,chd->ishd", mixed_rows, per_head, precision=PRECISE)
    gate_values = jax.nn.sigmoid(jnp.einsum("nsc,cd->nsd", normed, gate_weight, precision=PRECISE))
    gated_heads = gate_values * averaged.reshape(gate_values.shape)
    alignment_out = alignment + jnp.einsum(
        "nsd,dc->nsc", gated_heads, output_weight, precision=PRECISE
    )
    normed_out = normalize(alignment_out, outer_gain)
    left_side = jnp.einsum("nsc,cd->nsd", normed_out, left_weight, precision=PRECISE)
    right_side = jnp.einsum("nsc,cd->nsd", normed_out, right_weight, precision=PRECISE)
    factor_width = left_side.shape[2]
    columns = pair_state.shape[1]
    left_flat = left_side.transpose(1, 0, 2).reshape(local_seqs, local_rows * factor_width)
    right_rows = right_side.reshape(local_rows, local_seqs * factor_width)
    right_tokens = lax.all_gather(right_rows, "row", axis=0, tiled=True)
    right_tokens = right_tokens.reshape(-1, local_seqs, factor_width)
    right_columns = lax.all_to_all(right_tokens, "col", split_axis=0, concat_axis=1, tiled=True)
    right_all = right_columns.transpose(1, 0, 2)
    left_all = lax.all_gather(left_flat, "col", axis=0, tiled=True)
    sequences = left_all.shape[0]
    left_all = left_all.reshape(sequences, local_rows, factor_width)
    block_rows = 8
    left_blocks = left_all.reshape(
        sequences, local_rows // block_rows, block_rows, factor_width
    ).transpose(1, 2, 0, 3)

    def outer_block(left_block):
        product = jnp.einsum("isc,sjd->ijcd", left_block, right_all, precision=PRECISE) / sequences
        flattened = product.reshape(-1, factor_width * factor_width)
        projected = jnp.dot(
            flattened, outer_weight, precision=PRECISE, preferred_element_type=jnp.float32
        )
        return projected.reshape(block_rows, columns, -1)

    update = lax.map(outer_block, left_blocks).reshape(pair_state.shape)
    pair_out = pair_state + update + outer_bias
    return (alignment_out, pair_out)


def solution(mesh):
    return jax.shard_map(
        on_device,
        mesh=mesh,
        in_specs=(
            P("row", "col", None),
            P("row", "col", None),
            P(None, "row", "col"),
            P(),
            P(),
            P(),
            P(),
            P(),
            P(),
            P(),
            P(),
            P(),
        ),
        out_specs=(P("row", "col", None), P("row", "col", None)),
        check_vma=False,
    )
```

profile of v0, /device:TPU:0, one launch (start us, length us, event | category | flops | bytes accessed | tf_op | source)
XLA Modules:
  0.0 132.7 jit_solution(414286124162708641)
XLA Ops:
  0.6 0.0 copy-start
  0.7 1.0 reduce_sum.36
  1.7 1.0 multiply_reduce_fusion.1
  2.7 0.9 multiply_multiply_fusion.1
  3.6 0.1 reshape.65
  3.7 10.9 %all_gather.12 = f32[192,256]{1,0:T(8,128)S(1)} all-gather(f32[24,256]{1,0:T(8,128)S(1)} %reshape.65), channel_id=1, replica_groups=mesh['row'=8,'col'=4] {'row'}, dimensions={0}, use_global_device_ids=true | all-gather | bytes 221184 | tf_op jit(solution)/shard_map/all_gather | solution.py:36
  14.5 0.1 copy.88
  14.7 1.0 copy.89
  15.7 19.8 %all_gather.13 = f32[8,24,192]{1,0,2:T(8,128)S(1)} all-gather(f32[8,24,48]{1,0,2:T(8,128)S(1)} %copy.89), channel_id=1, replica_groups=mesh['row'=8,'col'=4] {'col'}, dimensions={2}, use_global_device_ids=true | all-gather | bytes 184320 | tf_op jit(solution)/shard_map/all_gather | solution.py:40
  35.5 0.9 copy.91
  36.5 1.5 %convolution_bitcast_fusion.2 = f32[24,4,8,64]{3,0,1,2:T(8,128)S(1)} fusion(f32[192,4,64,1]{0,2,1,3:T(8,128)S(1)} %bitcast.87, f32[8,24,192,1]{1,0,2,3:T(8,128)S(1)} %bitcast.83), kind=kOutput, calls=%fused_computation.8 | convolution fusion | flops 113246208 | bytes 540672 | tf_op jit(solution)/shard_map/hij,jsc->ishc/dot_general | solution.py:38
  38.0 0.5 convolution_bitcast_fusion.1
  38.5 0.2 copy.92
  38.7 0.2 reshape.68
  38.9 0.2 fusion.6
  39.2 0.3 fusion.21
  39.5 0.2 multiply_reduce_fusion
  39.7 0.2 fusion.12
  39.9 0.1 reshape.70
  40.0 9.2 %all_gather.15 = f32[192,128]{1,0:T(8,128)S(1)} all-gather(f32[24,128]{1,0:T(8,128)S(1)} %reshape.70), channel_id=1, replica_groups=mesh['row'=8,'col'=4] {'row'}, dimensions={0}, use_global_device_ids=true | all-gather | bytes 110592 | tf_op jit(solution)/shard_map/all_gather | solution.py:58
  49.3 0.1 copy.95
  49.4 0.2 copy.96
  49.6 0.9 reshape.87
  50.5 3.3 %all-to-all-start = ((f32[4,1,6144]{2,1,0:T(1,128)}), f32[4,1,6144]{2,1,0:T(1,128)S(1)}, u32[]{:S(2)}, u32[]{:S(2)}) async-start(f32[4,1,6144]{2,1,0:T(1,128)} %reshape.87), calls=%async_computation | async-start | bytes 196608 | tf_op jit(solution)/shard_map/all_to_all | solution.py:60
  53.8 0.6 copy.101
  54.4 0.2 convolution_bitcast_fusion.3
  54.7 0.1 reshape.73
  54.8 13.6 %all-gather = f32[4,4,768]{2,1,0:T(4,128)S(1)} all-gather(f32[1,4,768]{2,1,0:T(4,128)S(1)} %reshape.73), channel_id=1, replica_groups=mesh['row'=8,'col'=4] {'col'}, dimensions={0}, use_global_device_ids=true | all-gather | bytes 61440 | tf_op jit(solution)/shard_map/all_gather | solution.py:62
  68.4 0.1 reshape_reshape.3
  68.6 0.5 broadcast.66
  69.1 0.9 reduce
  70.0 0.2 reshape.88
  70.2 0.2 copy.98
  70.4 0.2 copy.100
  70.6 60.2 %while.10 = (s32[]{:T(128)}, f32[3,8,48,128]{3,2,1,0:T(8,128)}, f32[3,8,16,32]{3,1,0,2:T(8,128)S(1)}, f32[16,48,32]{1,0,2:T(8,128)S(1)}, f32[1024,128]{1,0:T(8,128)S(1)}, /*index=5*/s32[]{:T(128)}) while((s32[]{:T(128)}, f32[3,8,48,128]{3,2,1,0:T(8,128)}, f32[3,8,16,32]{3,1,0,2:T(8,128)S(1)}, f32[16,48,32]{1,0,2:T(8,128)S(1)}, ...), condition=%wide.region_5.6_spmd, body=%wide.region_4.5_spmd.sunk | while | flops 679870464 | bytes 10306121 | solution.py:78
  70.6 5.1 %multiply_bitcast_fusion.2 = f32[8,48,32,32]{1,2,3,0:T(8,128)} fusion(f32[16,48,32]{1,0,2:T(8,128)S(1)} %get-tuple-element.125, f32[1,8,16,32]{3,1,0,2:T(8,128)S(1)} %constant_dynamic-slice_fusion.2), kind=kOutput, calls=%fused_computation.clone.1 | convolution fusion | flops 75890688 | bytes 1687552 | tf_op jit(solution)/shard_map/while/body/eval_jaxpr/isc,sjd->ijcd/dot_general | solution.py:71
  75.7 7.9 %copy.122 = f32[8,48,32,32]{3,2,1,0:T(8,128)} copy(f32[8,48,32,32]{1,2,3,0:T(8,128)} %multiply_bitcast_fusion.2) | data formatting | bytes 3145728 | tf_op jit(solution)/shard_map/while/body/eval_jaxpr/div | solution.py:71
  83.5 5.0 %reshape.90 = f32[8,48,1024]{2,1,0:T(8,128)S(1)} reshape(f32[8,48,32,32]{3,2,1,0:T(8,128)} %copy.122) | data formatting | bytes 3145728 | tf_op jit(solution)/shard_map/reshape.27
  88.6 2.1 %fusion.34 = f32[3,8,48,128]{3,2,1,0:T(8,128)} fusion(f32[3,8,48,128]{3,2,1,0:T(8,128)} %get-tuple-element.117, s32[]{:T(128)} %get-tuple-element.116, f32[8,48,1024]{2,1,0:T(8,128)S(1)} %reshape.90, f32[1024,128]{1,0:T(8,128)S(1)} %get-tuple-element.126), kind=kOutput, calls=%fused_computation.2.clone.1 | convolution fusion | flops 603979776 | bytes 2294272 | tf_op jit(solution)/shard_map/while/body/eval_jaxpr/dot_general | solution.py:73
  90.7 5.1 %multiply_bitcast_fusion.2 = f32[8,48,32,32]{1,2,3,0:T(8,128)} fusion(f32[16,48,32]{1,0,2:T(8,128)S(1)} %get-tuple-element.125, f32[1,8,16,32]{3,1,0,2:T(8,128)S(1)} %constant_dynamic-slice_fusion.2), kind=kOutput, calls=%fused_computation.clone.1 | convolution fusion | flops 75890688 | bytes 1687552 | tf_op jit(solution)/shard_map/while/body/eval_jaxpr/isc,sjd->ijcd/dot_general | solution.py:71
  95.7 7.9 %copy.122 = f32[8,48,32,32]{3,2,1,0:T(8,128)} copy(f32[8,48,32,32]{1,2,3,0:T(8,128)} %multiply_bitcast_fusion.2) | data formatting | bytes 3145728 | tf_op jit(solution)/shard_map/while/body/eval_jaxpr/div | solution.py:71
  103.6 5.0 %reshape.90 = f32[8,48,1024]{2,1,0:T(8,128)S(1)} reshape(f32[8,48,32,32]{3,2,1,0:T(8,128)} %copy.122) | data formatting | bytes 3145728 | tf_op jit(solution)/shard_map/reshape.27
  108.6 2.1 %fusion.34 = f32[3,8,48,128]{3,2,1,0:T(8,128)} fusion(f32[3,8,48,128]{3,2,1,0:T(8,128)} %get-tuple-element.117, s32[]{:T(128)} %get-tuple-element.116, f32[8,48,1024]{2,1,0:T(8,128)S(1)} %reshape.90, f32[1024,128]{1,0:T(8,128)S(1)} %get-tuple-element.126), kind=kOutput, calls=%fused_computation.2.clone.1 | convolution fusion | flops 603979776 | bytes 2294272 | tf_op jit(solution)/shard_map/while/body/eval_jaxpr/dot_general | solution.py:73
  110.7 5.1 %multiply_bitcast_fusion.2 = f32[8,48,32,32]{1,2,3,0:T(8,128)} fusion(f32[16,48,32]{1,0,2:T(8,128)S(1)} %get-tuple-element.125, f32[1,8,16,32]{3,1,0,2:T(8,128)S(1)} %constant_dynamic-slice_fusion.2), kind=kOutput, calls=%fused_computation.clone.1 | convolution fusion | flops 75890688 | bytes 1687552 | tf_op jit(solution)/shard_map/while/body/eval_jaxpr/isc,sjd->ijcd/dot_general | solution.py:71
  115.8 7.9 %copy.122 = f32[8,48,32,32]{3,2,1,0:T(8,128)} copy(f32[8,48,32,32]{1,2,3,0:T(8,128)} %multiply_bitcast_fusion.2) | data formatting | bytes 3145728 | tf_op jit(solution)/shard_map/while/body/eval_jaxpr/div | solution.py:71
  123.6 5.0 %reshape.90 = f32[8,48,1024]{2,1,0:T(8,128)S(1)} reshape(f32[8,48,32,32]{3,2,1,0:T(8,128)} %copy.122) | data formatting | bytes 3145728 | tf_op jit(solution)/shard_map/reshape.27
  128.7 2.1 %fusion.34 = f32[3,8,48,128]{3,2,1,0:T(8,128)} fusion(f32[3,8,48,128]{3,2,1,0:T(8,128)} %get-tuple-element.117, s32[]{:T(128)} %get-tuple-element.116, f32[8,48,1024]{2,1,0:T(8,128)S(1)} %reshape.90, f32[1024,128]{1,0:T(8,128)S(1)} %get-tuple-element.126), kind=kOutput, calls=%fused_computation.2.clone.1 | convolution fusion | flops 603979776 | bytes 2294272 | tf_op jit(solution)/shard_map/while/body/eval_jaxpr/dot_general | solution.py:73
  130.8 1.9 %fusion.8 = f32[24,48,128]{2,1,0:T(8,128)} fusion(f32[24,48,128]{2,1,0:T(8,128)S(1)} %copy-done.3, f32[3,8,48,128]{3,2,1,0:T(8,128)} %get-tuple-element.29, f32[128]{0:T(128)S(1)} %copy-done.5), kind=kLoop, calls=%fused_computation.18 | loop fusion | flops 294912 | bytes 1769984 | tf_op jit(solution)/shard_map/add | solution.py:79
  (27 shorter events, 0.1 us)
Async XLA Ops:
  0.6 38.3 %copy-start = (f32[64,256]{1,0:T(8,128)S(1)}, f32[64,256]{1,0:T(8,128)}, u32[]{:S(2)}) copy-start(f32[64,256]{1,0:T(8,128)} %param.19) | copy-start | bytes 196612
  0.6 38.5 %copy-start.2 = (f32[24,4,64]{2,1,0:T(4,128)S(1)}, f32[24,4,64]{2,1,0:T(4,128)}, u32[]{:S(2)}) copy-start(f32[24,4,64]{2,1,0:T(4,128)} %param.14) | copy-start | bytes 73732
  0.7 38.5 %copy-start.4 = (f32[256,64]{0,1:T(8,128)S(1)}, f32[256,64]{0,1:T(8,128)}, u32[]{:S(2)}) copy-start(f32[256,64]{0,1:T(8,128)} %param.20) | copy-start | bytes 196612
  0.7 39.0 %copy-start.8 = (f32[64]{0:T(128)S(1)}, f32[64]{0:T(128)}, u32[]{:S(2)}) copy-start(f32[64]{0:T(128)} %param.21) | copy-start | bytes 772
  0.7 39.0 %copy-start.6 = (f32[64,32]{0,1:T(8,128)S(1)}, f32[64,32]{0,1:T(8,128)}, u32[]{:S(2)}) copy-start(f32[64,32]{0,1:T(8,128)} %param.23) | copy-start | bytes 24580
  3.7 50.8 %copy-start.7 = (f32[64,32]{0,1:T(8,128)S(1)}, f32[64,32]{0,1:T(8,128)}, u32[]{:S(2)}) copy-start(f32[64,32]{0,1:T(8,128)} %param.22) | copy-start | bytes 24580
  36.5 34.1 %copy-start.1 = (f32[1024,128]{1,0:T(8,128)S(1)}, f32[1024,128]{1,0:T(8,128)}, u32[]{:S(2)}) copy-start(f32[1024,128]{1,0:T(8,128)} %param.24) | copy-start | bytes 1572868
  50.5 18.1 %all-to-all-start = ((f32[4,1,6144]{2,1,0:T(1,128)}), f32[4,1,6144]{2,1,0:T(1,128)S(1)}, u32[]{:S(2)}, u32[]{:S(2)}) async-start(f32[4,1,6144]{2,1,0:T(1,128)} %reshape.87), calls=%async_computation | async-start | bytes 196608 | tf_op jit(solution)/shard_map/all_to_all | solution.py:60
  70.5 60.2 %copy-start.3 = (f32[24,48,128]{2,1,0:T(8,128)S(1)}, f32[24,48,128]{2,1,0:T(8,128)}, u32[]{:S(2)}) copy-start(f32[24,48,128]{2,1,0:T(8,128)} %param.15) | copy-start | bytes 1769476
  70.5 60.2 %copy-start.5 = (f32[128]{0:T(128)S(1)}, f32[128]{0:T(128)}, u32[]{:S(2)}) copy-start(f32[128]{0:T(128)} %param.25) | copy-start | bytes 1540
where the time goes:
time: 134 us; the launch traced here: 133 us
  blocking collectives  53.6 us (40%)
  local copies, waits for them, and re-layouts  44.6 us (33%)
  matrix products  24.4 us (18%)
  other arithmetic  5.88 us (4%)
  starting transfers between devices  3.3 us (2%)
    div x3, local copies, waits for them, and re-layouts, outer_block(): jnp.einsum('isc,sjd->ijcd', left_block, right_all, precision=PRECISE)  23.6 us
    all_gather x1, blocking collectives, on_device(): lax.all_gather(pair_weights, 'col', axis=2, tiled=True)  19.8 us
    dot_general x3, matrix products, outer_block(): jnp.einsum('isc,sjd->ijcd', left_block, right_all, precision=PRECISE)  15.2 us
    another operation x3, local copies, waits for them, and re-layouts  15.1 us
    all_gather x1, blocking collectives, on_device(): left_all = lax.all_gather(left_flat, 'col', axis=0, tiled=True)  13.6 us
    all_gather x1, blocking collectives, on_device(): gathered = lax.all_gather(flat_normed, 'row', axis=0, tiled=True)  10.9 us
    all_gather x1, blocking collectives, on_device(): right_tokens = lax.all_gather(right_rows, 'row', axis=0, tiled=True)  9.21 us
    dot_general x3, matrix products, outer_block(): jnp.dot(flattened, outer_weight, precision=PRECISE, preferred_element_typ...  6.23 us
  transfers between devices with their start and end apart: 1, of which 0 were waited for; matrix products, arithmetic and copies ran while one was open for 1% of the time, Pallas kernels for 0%

commit v1 on v0

--- a/solution.py
+++ b/solution.py
@@ -35,12 +35,20 @@
     flat_normed = normed.reshape(local_rows, local_seqs * channels)
     gathered = lax.all_gather(flat_normed, "row", axis=0, tiled=True)
     gathered = gathered.reshape(-1, local_seqs, channels)
-    mixed_rows = jnp.einsum(
-        "hij,jsc->ishc",
-        lax.all_gather(pair_weights, "col", axis=2, tiled=True),
-        gathered,
-        precision=PRECISE,
-    )
+    size, mine, rows = (lax.axis_size("col"), lax.axis_index("col"), pair_weights.shape[2])
+    forward = [(i, (i + 1) % size) for i in range(size)]
+    block, so_far = (pair_weights, None)
+    for turn in range(size):
+        arriving = lax.ppermute(block, "col", forward) if turn < size - 1 else None
+        absorb = jnp.einsum(
+            "hij,jsc->ishc",
+            block,
+            lax.dynamic_slice_in_dim(gathered, (mine - turn) % size * rows, block.shape[2], axis=0),
+            precision=PRECISE,
+        )
+        so_far = absorb if so_far is None else so_far + absorb
+        block = arriving
+    mixed_rows = so_far
     per_head = value_weight.reshape(channels, head_count, -1)
     averaged = jnp.einsum("ishc,chd->ishd", mixed_rows, per_head, precision=PRECISE)
     gate_values = jax.nn.sigmoid(jnp.einsum("nsc,cd->nsd", normed, gate_weight, precision=PRECISE))

time: 134 us -> 128 us (0.955)
  blocking collectives: 53.6 us -> 32.2 us
  waiting for transfers between devices: 0.01 us -> 10.5 us
  starting transfers between devices: 3.3 us -> 8.04 us
  matrix products: 24.4 us -> 26.1 us
    all_gather x1 -> x0, blocking collectives: 19.8 us -> none  [on_device(): lax.all_gather(pair_weights, 'col', axis=2, tiled=True)]
    ppermute x0 -> x3, waiting for transfers between devices: none -> 10.5 us  [on_device(): arriving = lax.ppermute(block, 'col', forward) if turn < size - 1 else None]
    ppermute x0 -> x3, starting transfers between devices: none -> 4.74 us  [on_device(): arriving = lax.ppermute(block, 'col', forward) if turn < size - 1 else None]
    dot_general x1 -> x4, matrix products: 1.51 us -> 3.22 us  [on_device(): jnp.einsum('hij,jsc->ishc', block, lax.dynamic_slice_in_dim(gathered, (mi...]
    all_gather x1, blocking collectives: 10.9 us -> 9.25 us  [on_device(): gathered = lax.all_gather(flat_normed, 'row', axis=0, tiled=True)]
    unnamed x24 -> x23, local copies, waits for them, and re-layouts: 3.85 us -> 2.85 us
  transfers between devices with their start and end apart: 1 -> 4, of which waited for: 0 -> 2; matrix products, arithmetic and copies ran while one was open for 1% -> 6% of each run, Pallas kernels for 0% -> 0%
where the time goes in v1:
time: 128 us; the launch traced here: 127 us
  local copies, waits for them, and re-layouts  43.5 us (34%)
  blocking collectives  32.2 us (25%)
  matrix products  26.1 us (20%)
  waiting for transfers between devices  10.5 us (8%)
  starting transfers between devices  8.04 us (6%)
  other arithmetic  5.8 us (5%)
    div x3, local copies, waits for them, and re-layouts, outer_block(): jnp.einsum('isc,sjd->ijcd', left_block, right_all, precision=PRECISE)  23.6 us
    dot_general x3, matrix products, outer_block(): jnp.einsum('isc,sjd->ijcd', left_block, right_all, precision=PRECISE)  15.1 us
    another operation x3, local copies, waits for them, and re-layouts  15.1 us
    all_gather x1, blocking collectives, on_device(): left_all = lax.all_gather(left_flat, 'col', axis=0, tiled=True)  13.8 us
    ppermute x3, waiting for transfers between devices, on_device(): arriving = lax.ppermute(block, 'col', forward) if turn < size - 1 else None  10.5 us
    all_gather x1, blocking collectives, on_device(): gathered = lax.all_gather(flat_normed, 'row', axis=0, tiled=True)  9.25 us
    all_gather x1, blocking collectives, on_device(): right_tokens = lax.all_gather(right_rows, 'row', axis=0, tiled=True)  9.22 us
    dot_general x3, matrix products, outer_block(): jnp.dot(flattened, outer_weight, precision=PRECISE, preferred_element_typ...  6.24 us
  transfers between devices with their start and end apart: 4, of which 2 were waited for; matrix products, arithmetic and copies ran while one was open for 6% of the time, Pallas kernels for 0%

profile of v1, /device:TPU:0, one launch (start us, length us, event | category | flops | bytes accessed | tf_op | source)
XLA Modules:
  0.0 127.3 jit_solution(948435919497873984)
XLA Ops:
  0.7 3.1 %collective-permute-start = (f32[8,24,48]{2,1,0:T(8,128)}, f32[8,24,48]{2,1,0:T(8,128)S(1)}, u32[]{:S(2)}, u32[]{:S(2)}) collective-permute-start(f32[8,24,48]{2,1,0:T(8,128)} %param.16), channel_id=1, source_target_pairs={{0,1},{1,2},{2,3},{3,0},{4,5},{5,6},{6,7},{7,4},{8,9},{9,10},{10,1... | collective-permute-start | bytes 110600 | tf_op jit(solution)/shard_map/ppermute | solution.py:42
  3.8 0.9 reduce_sum.36
  4.7 1.0 multiply_reduce_fusion.1
  5.7 0.9 multiply_multiply_fusion.1
  6.7 9.3 %all_gather.9 = f32[192,256]{1,0:T(8,128)S(1)} all-gather(f32[24,256]{1,0:T(8,128)S(1)} %reshape.65), channel_id=1, replica_groups=mesh['row'=8,'col'=4] {'row'}, dimensions={0}, use_global_device_ids=true | all-gather | bytes 221184 | tf_op jit(solution)/shard_map/all_gather | solution.py:36
  16.0 0.1 copy.96
  16.1 1.5 %fusion.12 = f32[4,64,8,24]{1,3,0,2:T(8,128)S(1)} fusion(f32[192,4,64]{0,2,1:T(8,128)S(1)} %bitcast.115, s32[]{:T(128)S(6)} %select_n.32, f32[8,24,48]{2,1,0:T(8,128)} %param.16), kind=kOutput, calls=%fused_computation.24 | convolution fusion | flops 28311552 | bytes 364548 | tf_op jit(solution)/shard_map/hij,jsc->ishc/dot_general | solution.py:43
  17.7 0.9 copy.101
  18.6 1.6 %collective-permute-start.1 = (f32[8,24,48]{2,1,0:T(8,128)S(1)}, f32[8,24,48]{2,1,0:T(8,128)S(1)}, u32[]{:S(2)}, u32[]{:S(2)}) collective-permute-start(f32[8,24,48]{2,1,0:T(8,128)S(1)} %collective-permute-done), channel_id=1, source_target_pairs={{0,1},{1,2},{2,3},{3,0},{4,5},{5,6},{6,7},{7,4},{8,9},{9,10},{10,1... | collective-permute-start | bytes 110600 | tf_op jit(solution)/shard_map/ppermute | solution.py:42
  20.3 0.6 convolution_add_fusion.2
  20.9 4.7 %collective-permute-done.1 = f32[8,24,48]{2,1,0:T(8,128)S(1)} collective-permute-done((f32[8,24,48]{2,1,0:T(8,128)S(1)}, f32[8,24,48]{2,1,0:T(8,128)S(1)}, u32[]{:S(2)}, u32[]{:S(2)}) %collective-permute-start.1) | collective-permute-done | bytes 36896 | tf_op jit(solution)/shard_map/ppermute | solution.py:42
  25.5 0.6 convolution_add_fusion.1
  26.1 5.8 %collective-permute-done.2 = f32[8,24,48]{2,1,0:T(8,128)S(1)} collective-permute-done((f32[8,24,48]{2,1,0:T(8,128)S(1)}, f32[8,24,48]{2,1,0:T(8,128)S(1)}, u32[]{:S(2)}, u32[]{:S(2)}) %collective-permute-start.2) | collective-permute-done | bytes 36896 | tf_op jit(solution)/shard_map/ppermute | solution.py:42
  32.0 0.6 fusion.3
  32.5 0.5 convolution_bitcast_fusion.1
  33.0 0.2 copy.102
  33.3 0.2 reshape.68
  33.4 0.2 fusion.7
  33.7 0.3 fusion.38
  34.0 0.6 copy.111
  34.7 0.2 multiply_reduce_fusion
  34.9 0.2 fusion.25
  35.2 9.2 %all_gather.11 = f32[192,128]{1,0:T(8,128)S(1)} all-gather(f32[24,128]{1,0:T(8,128)S(1)} %reshape.70), channel_id=1, replica_groups=mesh['row'=8,'col'=4] {'row'}, dimensions={0}, use_global_device_ids=true | all-gather | bytes 110592 | tf_op jit(solution)/shard_map/all_gather | solution.py:66
  44.5 0.2 copy.106
  44.7 0.9 reshape.93
  45.7 3.3 %all-to-all-start = ((f32[4,1,6144]{2,1,0:T(1,128)}), f32[4,1,6144]{2,1,0:T(1,128)S(1)}, u32[]{:S(2)}, u32[]{:S(2)}) async-start(f32[4,1,6144]{2,1,0:T(1,128)} %reshape.93), calls=%async_computation | async-start | bytes 196608 | tf_op jit(solution)/shard_map/all_to_all | solution.py:68
  49.0 0.2 convolution_bitcast_fusion.2
  49.3 13.8 %all-gather = f32[4,4,768]{2,1,0:T(4,128)S(1)} all-gather(f32[1,4,768]{2,1,0:T(4,128)S(1)} %reshape.73), channel_id=1, replica_groups=mesh['row'=8,'col'=4] {'col'}, dimensions={0}, use_global_device_ids=true | all-gather | bytes 61440 | tf_op jit(solution)/shard_map/all_gather | solution.py:70
  63.1 0.1 reshape_reshape.3
  63.2 0.5 broadcast.70
  63.7 0.9 reduce
  64.6 0.2 reshape.94
  64.9 0.2 copy.108
  65.0 0.2 copy.110
  65.2 60.1 %while.10 = (s32[]{:T(128)}, f32[3,8,48,128]{3,2,1,0:T(8,128)}, f32[3,8,16,32]{3,1,0,2:T(8,128)S(1)}, f32[16,48,32]{1,0,2:T(8,128)S(1)}, f32[1024,128]{1,0:T(8,128)S(1)}, /*index=5*/s32[]{:T(128)}) while((s32[]{:T(128)}, f32[3,8,48,128]{3,2,1,0:T(8,128)}, f32[3,8,16,32]{3,1,0,2:T(8,128)S(1)}, f32[16,48,32]{1,0,2:T(8,128)S(1)}, ...), condition=%wide.region_5.6_spmd, body=%wide.region_4.5_spmd.sunk | while | flops 679870464 | bytes 10306121 | solution.py:86
  65.3 5.1 %multiply_bitcast_fusion.2 = f32[8,48,32,32]{1,2,3,0:T(8,128)} fusion(f32[16,48,32]{1,0,2:T(8,128)S(1)} %get-tuple-element.125, f32[1,8,16,32]{3,1,0,2:T(8,128)S(1)} %constant_dynamic-slice_fusion.2), kind=kOutput, calls=%fused_computation.clone.1 | convolution fusion | flops 75890688 | bytes 1687552 | tf_op jit(solution)/shard_map/while/body/eval_jaxpr/isc,sjd->ijcd/dot_general | solution.py:79
  70.3 7.9 %copy.135 = f32[8,48,32,32]{3,2,1,0:T(8,128)} copy(f32[8,48,32,32]{1,2,3,0:T(8,128)} %multiply_bitcast_fusion.2) | data formatting | bytes 3145728 | tf_op jit(solution)/shard_map/while/body/eval_jaxpr/div | solution.py:79
  78.2 5.0 %reshape.96 = f32[8,48,1024]{2,1,0:T(8,128)S(1)} reshape(f32[8,48,32,32]{3,2,1,0:T(8,128)} %copy.135) | data formatting | bytes 3145728 | tf_op jit(solution)/shard_map/reshape.27
  83.2 2.1 %fusion.50 = f32[3,8,48,128]{3,2,1,0:T(8,128)} fusion(f32[3,8,48,128]{3,2,1,0:T(8,128)} %get-tuple-element.117, s32[]{:T(128)} %get-tuple-element.116, f32[8,48,1024]{2,1,0:T(8,128)S(1)} %reshape.96, f32[1024,128]{1,0:T(8,128)S(1)} %get-tuple-element.126), kind=kOutput, calls=%fused_computation.2.clone.1 | convolution fusion | flops 603979776 | bytes 2294272 | tf_op jit(solution)/shard_map/while/body/eval_jaxpr/dot_general | solution.py:81
  85.3 5.0 %multiply_bitcast_fusion.2 = f32[8,48,32,32]{1,2,3,0:T(8,128)} fusion(f32[16,48,32]{1,0,2:T(8,128)S(1)} %get-tuple-element.125, f32[1,8,16,32]{3,1,0,2:T(8,128)S(1)} %constant_dynamic-slice_fusion.2), kind=kOutput, calls=%fused_computation.clone.1 | convolution fusion | flops 75890688 | bytes 1687552 | tf_op jit(solution)/shard_map/while/body/eval_jaxpr/isc,sjd->ijcd/dot_general | solution.py:79
  90.4 7.9 %copy.135 = f32[8,48,32,32]{3,2,1,0:T(8,128)} copy(f32[8,48,32,32]{1,2,3,0:T(8,128)} %multiply_bitcast_fusion.2) | data formatting | bytes 3145728 | tf_op jit(solution)/shard_map/while/body/eval_jaxpr/div | solution.py:79
  98.2 5.0 %reshape.96 = f32[8,48,1024]{2,1,0:T(8,128)S(1)} reshape(f32[8,48,32,32]{3,2,1,0:T(8,128)} %copy.135) | data formatting | bytes 3145728 | tf_op jit(solution)/shard_map/reshape.27
  103.3 2.1 %fusion.50 = f32[3,8,48,128]{3,2,1,0:T(8,128)} fusion(f32[3,8,48,128]{3,2,1,0:T(8,128)} %get-tuple-element.117, s32[]{:T(128)} %get-tuple-element.116, f32[8,48,1024]{2,1,0:T(8,128)S(1)} %reshape.96, f32[1024,128]{1,0:T(8,128)S(1)} %get-tuple-element.126), kind=kOutput, calls=%fused_computation.2.clone.1 | convolution fusion | flops 603979776 | bytes 2294272 | tf_op jit(solution)/shard_map/while/body/eval_jaxpr/dot_general | solution.py:81
  105.3 5.0 %multiply_bitcast_fusion.2 = f32[8,48,32,32]{1,2,3,0:T(8,128)} fusion(f32[16,48,32]{1,0,2:T(8,128)S(1)} %get-tuple-element.125, f32[1,8,16,32]{3,1,0,2:T(8,128)S(1)} %constant_dynamic-slice_fusion.2), kind=kOutput, calls=%fused_computation.clone.1 | convolution fusion | flops 75890688 | bytes 1687552 | tf_op jit(solution)/shard_map/while/body/eval_jaxpr/isc,sjd->ijcd/dot_general | solution.py:79
  110.4 7.9 %copy.135 = f32[8,48,32,32]{3,2,1,0:T(8,128)} copy(f32[8,48,32,32]{1,2,3,0:T(8,128)} %multiply_bitcast_fusion.2) | data formatting | bytes 3145728 | tf_op jit(solution)/shard_map/while/body/eval_jaxpr/div | solution.py:79
  118.3 5.0 %reshape.96 = f32[8,48,1024]{2,1,0:T(8,128)S(1)} reshape(f32[8,48,32,32]{3,2,1,0:T(8,128)} %copy.135) | data formatting | bytes 3145728 | tf_op jit(solution)/shard_map/reshape.27
  123.3 2.1 %fusion.50 = f32[3,8,48,128]{3,2,1,0:T(8,128)} fusion(f32[3,8,48,128]{3,2,1,0:T(8,128)} %get-tuple-element.117, s32[]{:T(128)} %get-tuple-element.116, f32[8,48,1024]{2,1,0:T(8,128)S(1)} %reshape.96, f32[1024,128]{1,0:T(8,128)S(1)} %get-tuple-element.126), kind=kOutput, calls=%fused_computation.2.clone.1 | convolution fusion | flops 603979776 | bytes 2294272 | tf_op jit(solution)/shard_map/while/body/eval_jaxpr/dot_general | solution.py:81
  125.4 1.9 %fusion.8 = f32[24,48,128]{2,1,0:T(8,128)} fusion(f32[24,48,128]{2,1,0:T(8,128)S(1)} %copy-done.3, f32[3,8,48,128]{3,2,1,0:T(8,128)} %get-tuple-element.29, f32[128]{0:T(128)S(1)} %copy-done.5), kind=kLoop, calls=%fused_computation.20 | loop fusion | flops 294912 | bytes 1769984 | tf_op jit(solution)/shard_map/add | solution.py:87
  (34 shorter events, 0.5 us)
Async XLA Ops:
  0.6 32.8 %copy-start = (f32[64,256]{1,0:T(8,128)S(1)}, f32[64,256]{1,0:T(8,128)}, u32[]{:S(2)}) copy-start(f32[64,256]{1,0:T(8,128)} %param.19) | copy-start | bytes 196612
  0.6 33.0 %copy-start.2 = (f32[24,4,64]{2,1,0:T(4,128)S(1)}, f32[24,4,64]{2,1,0:T(4,128)}, u32[]{:S(2)}) copy-start(f32[24,4,64]{2,1,0:T(4,128)} %param.14) | copy-start | bytes 73732
  0.7 33.0 %copy-start.4 = (f32[256,64]{0,1:T(8,128)S(1)}, f32[256,64]{0,1:T(8,128)}, u32[]{:S(2)}) copy-start(f32[256,64]{0,1:T(8,128)} %param.20) | copy-start | bytes 196612
  0.7 34.2 %copy-start.8 = (f32[64]{0:T(128)S(1)}, f32[64]{0:T(128)}, u32[]{:S(2)}) copy-start(f32[64]{0:T(128)} %param.21) | copy-start | bytes 772
  0.7 34.2 %copy-start.6 = (f32[64,32]{0,1:T(8,128)S(1)}, f32[64,32]{0,1:T(8,128)}, u32[]{:S(2)}) copy-start(f32[64,32]{0,1:T(8,128)} %param.23) | copy-start | bytes 24580
  0.7 17.9 %collective-permute-start = (f32[8,24,48]{2,1,0:T(8,128)}, f32[8,24,48]{2,1,0:T(8,128)S(1)}, u32[]{:S(2)}, u32[]{:S(2)}) collective-permute-start(f32[8,24,48]{2,1,0:T(8,128)} %param.16), channel_id=1, source_target_pairs={{0,1},{1,2},{2,3},{3,0},{4,5},{5,6},{6,7},{7,4},{8,9},{9,10},{10,1... | collective-permute-start | bytes 110600 | tf_op jit(solution)/shard_map/ppermute | solution.py:42
  17.6 31.4 %copy-start.7 = (f32[64,32]{0,1:T(8,128)S(1)}, f32[64,32]{0,1:T(8,128)}, u32[]{:S(2)}) copy-start(f32[64,32]{0,1:T(8,128)} %param.22) | copy-start | bytes 24580
  18.6 6.9 %collective-permute-start.1 = (f32[8,24,48]{2,1,0:T(8,128)S(1)}, f32[8,24,48]{2,1,0:T(8,128)S(1)}, u32[]{:S(2)}, u32[]{:S(2)}) collective-permute-start(f32[8,24,48]{2,1,0:T(8,128)S(1)} %collective-permute-done), channel_id=1, source_target_pairs={{0,1},{1,2},{2,3},{3,0},{4,5},{5,6},{6,7},{7,4},{8,9},{9,10},{10,1... | collective-permute-start | bytes 110600 | tf_op jit(solution)/shard_map/ppermute | solution.py:42
  25.5 6.4 %collective-permute-start.2 = (f32[8,24,48]{2,1,0:T(8,128)S(1)}, f32[8,24,48]{2,1,0:T(8,128)S(1)}, u32[]{:S(2)}, u32[]{:S(2)}) collective-permute-start(f32[8,24,48]{2,1,0:T(8,128)S(1)} %collective-permute-done.1), channel_id=1, source_target_pairs={{0,1},{1,2},{2,3},{3,0},{4,5},{5,6},{6,7},{7,4},{8,9},{9,10},{10,1... | collective-permute-start | bytes 110600 | tf_op jit(solution)/shard_map/ppermute | solution.py:42
  26.1 39.1 %copy-start.1 = (f32[1024,128]{1,0:T(8,128)S(1)}, f32[1024,128]{1,0:T(8,128)}, u32[]{:S(2)}) copy-start(f32[1024,128]{1,0:T(8,128)} %param.24) | copy-start | bytes 1572868
  45.7 17.5 %all-to-all-start = ((f32[4,1,6144]{2,1,0:T(1,128)}), f32[4,1,6144]{2,1,0:T(1,128)S(1)}, u32[]{:S(2)}, u32[]{:S(2)}) async-start(f32[4,1,6144]{2,1,0:T(1,128)} %reshape.93), calls=%async_computation | async-start | bytes 196608 | tf_op jit(solution)/shard_map/all_to_all | solution.py:68
  65.2 60.2 %copy-start.3 = (f32[24,48,128]{2,1,0:T(8,128)S(1)}, f32[24,48,128]{2,1,0:T(8,128)}, u32[]{:S(2)}) copy-start(f32[24,48,128]{2,1,0:T(8,128)} %param.15) | copy-start | bytes 1769476
  65.2 60.2 %copy-start.5 = (f32[128]{0:T(128)S(1)}, f32[128]{0:T(128)}, u32[]{:S(2)}) copy-start(f32[128]{0:T(128)} %param.25) | copy-start | bytes 1540
